TPU v7x, 32 devices: a whole 2x2x4 slice. The times are simulated.
32 devices in a mesh: seq: 8 (over y, x, core), tp: 4 (over z).
Axes of the slice: x: 2, y: 2, z: 4, core: 2. Of those that a mesh axis runs over, the one named last changes fastest.
Arguments:
- grad_out: bfloat16 [1024, 8192], P('seq', 'tp'), may hold values from -6 to 6
- resid_in: bfloat16 [1024, 8192], P('seq', 'tp'), may hold values from -6 to 6
- down_weight: bfloat16 [28672, 8192], P('seq', 'tp'), may hold values from -0.03125 to 0.03125
- hidden_clean: bfloat16 [28672, 512], P('seq', 'tp'), may hold values from -6 to 6
- hidden_corrupt: bfloat16 [28672, 512], P('seq', 'tp'), may hold values from -6 to 6
- patched: int32 [14336], replicated, may hold values from 0 to 28671, as said below
Outputs:
- resid_scores: float32 [1024], P('seq')
- token_scores: float32 [512], P('tp')
- neuron_scores: float32 [28672], P('seq')
Inputs may be any that keep to these rules, and one draw needn't show every extreme that they name: `patched`: 14336 distinct hidden-unit indices.
All inputs are finite; a program needn't handle non-finite values.
Results may differ from a plain program's by a relative error of at most 0.0046.
Values may be sent and summed in bfloat16 or wider, within the bound.
A program may use at most 128 MiB of HBM per device.

v0:
```python
import math
import jax
import jax.numpy as jnp
from jax import lax
from jax.sharding import PartitionSpec as P


def from_behind(value, axis, steps):
    count = lax.axis_size(axis)
    pairs = [(source, (source + steps) % count) for source in range(count)]
    return lax.ppermute(value, axis, pairs)


def patch_mask(patched, unit_rows):
    lanes = math.gcd(unit_rows, 128)
    groups = unit_rows // lanes
    local = patched - lax.axis_index("seq") * unit_rows
    high = local[None, :] // lanes == jnp.arange(groups, dtype=jnp.int32)[:, None]
    high = high & (local >= 0)[None, :]
    low = (local % lanes)[:, None] == jnp.arange(lanes, dtype=jnp.int32)[None, :]
    counts = lax.dot_general(
        high.astype(jnp.bfloat16),
        low.astype(jnp.bfloat16),
        (((1,), (0,)), ((), ())),
        preferred_element_type=jnp.float32,
    )
    return counts.reshape(unit_rows)


def shards(grad_out, resid_in, down_weight, hidden_clean, hidden_corrupt, patched):
    seq_count = lax.axis_size("seq")
    tp_count = lax.axis_size("tp")
    pair_count = seq_count // 2
    half_rows = grad_out.shape[0] // 2
    unit_rows = down_weight.shape[0]
    model_width = resid_in.shape[1] * tp_count
    hidden_diff = (hidden_clean.astype(jnp.float32) - hidden_corrupt.astype(jnp.float32)).astype(
        jnp.bfloat16
    )
    diff_all = lax.all_gather(hidden_diff, "tp", axis=0)
    in_upper = lax.axis_index("seq") // pair_count
    send_start = (1 - in_upper) * half_rows
    keep_start = in_upper * half_rows
    sent_grad = lax.dynamic_slice_in_dim(grad_out, send_start, half_rows, 0)
    partner_grad = from_behind(sent_grad, "seq", pair_count)
    partner_resid = from_behind(resid_in, "seq", pair_count)
    sign_factor = (1 - 2 * in_upper).astype(jnp.float32)
    resid_diff = sign_factor * (resid_in.astype(jnp.float32) - partner_resid.astype(jnp.float32))
    resid_part = jnp.sum(resid_diff * grad_out.astype(jnp.float32), axis=1)
    kept_grad = lax.dynamic_slice_in_dim(grad_out, keep_start, half_rows, 0)
    grad_mean = ((kept_grad.astype(jnp.float32) + partner_grad.astype(jnp.float32)) * 0.5).astype(
        jnp.bfloat16
    )
    grads = lax.all_gather(grad_mean, "seq", axis=0)
    width = grads.shape[-1]
    grads = grads.reshape(2, pair_count, half_rows, width).transpose(1, 0, 2, 3)
    grads = grads.reshape(-1, width)
    total_len = grads.shape[0]
    in_patch = patch_mask(patched, unit_rows)
    unit_grad = lax.dot_general(
        down_weight, grads, (((1,), (1,)), ((), ())), preferred_element_type=jnp.float32
    )
    local_len = total_len // tp_count
    token_parts = []
    unit_part = 0.0
    for block in range(tp_count):
        part = unit_grad[:, block * local_len : (block + 1) * local_len]
        product = diff_all[block].astype(jnp.float32) * part
        token_parts.append(jnp.sum(product * in_patch[:, None], axis=0))
        unit_part = unit_part + jnp.sum(product, axis=1)
    token_part = jnp.stack(token_parts)
    token_total = lax.psum(token_part, ("seq", "tp"))
    token_mine = lax.dynamic_index_in_dim(token_total, lax.axis_index("tp"), 0, keepdims=False)
    token_scores = token_mine / math.sqrt(patched.shape[0])
    unit_total, resid_total = lax.psum((unit_part, resid_part), "tp")
    neuron_scores = unit_total / math.sqrt(total_len)
    resid_scores = resid_total / math.sqrt(model_width)
    return (resid_scores, token_scores, neuron_scores)


def solution(mesh):
    in_specs = (P("seq", "tp"), P("seq", "tp"), P("seq", "tp"), P("seq", "tp"), P("seq", "tp"), P())
    out_specs = (P("seq"), P("tp"), P("seq"))
    return jax.shard_map(shards, mesh=mesh, in_specs=in_specs, out_specs=out_specs, check_vma=False)
```

profile of v0, /device:TPU:10, one launch (start us, length us, event | category | flops | bytes accessed | tf_op | source)
XLA Modules:
  0.0 192.9 jit_solution(12017848095058334556)
XLA Ops:
  7.3 1.1 constant_dynamic-slice_fusion.1
  8.3 1.6 collective-permute-start.1
  9.9 6.5 %collective-permute-done.1 = bf16[64,2048]{1,0:T(8,128)(2,1)S(1)} collective-permute-done((bf16[64,2048]{1,0:T(8,128)(2,1)S(1)}, bf16[64,2048]{1,0:T(8,128)(2,1)S(1)}, u32[]{:S(2)}, u32[]{:S(2)}) %collective-permute-start.1) | collective-permute-done | bytes 262176 | tf_op jit(solution)/shard_map/ppermute | solution.py:11
  16.5 1.8 multiply_convert_fusion
  18.2 0.0 all-gather.5.cloned.1.call-start
  18.3 1.6 collective-permute-start
  19.9 0.5 copy.14
  20.4 0.5 copy.13
  20.9 1.1 subtract_convert_fusion
  22.1 0.1 add_select_fusion.1
  22.2 0.3 fusion.22
  22.6 2.1 %fusion.8 = f32[3584]{0:T(1024)S(1)} fusion(s32[14336]{0:T(1024)S(1)} %get-tuple-element.18, pred[28,14336]{1,0:T(8,128)(4,1)S(1)} %fusion.22), kind=kOutput, calls=%fused_computation.19 | convolution fusion | flops 104595456 | bytes 473088 | tf_op jit(solution)/shard_map/dot_general | solution.py:21
  24.7 9.5 %collective-permute-done = bf16[128,2048]{1,0:T(8,128)(2,1)S(1)} collective-permute-done((bf16[128,2048]{1,0:T(8,128)(2,1)}, bf16[128,2048]{1,0:T(8,128)(2,1)S(1)}, u32[]{:S(2)}, u32[]{:S(2)}) %collective-permute-start) | collective-permute-done | bytes 524320 | tf_op jit(solution)/shard_map/ppermute | solution.py:11
  34.2 0.3 multiply_reduce_fusion.4
  34.5 14.7 %all-gather.7.cloned.1.call-done = bf16[512,2048]{1,0:T(8,128)(2,1)} async-done(((bf16[64,2048]{1,0:T(8,128)(2,1)}), bf16[512,2048]{1,0:T(8,128)(2,1)}) %all-gather.7.cloned.1.call-update) | async-done | bytes 2097168 | tf_op jit(solution)/shard_map/all_gather | solution.py:54
  49.2 1.7 copy.15
  51.0 13.1 %convolution_bitcast_fusion = f32[3584,512]{0,1:T(8,128)} fusion(bf16[512,2048]{1,0:T(8,128)(2,1)S(1)} %bitcast.20, bf16[3584,2048]{1,0:T(8,128)(2,1)} %param.8), kind=kOutput, calls=%fused_computation.2 | convolution fusion | flops 7516192768 | bytes 24117248 | tf_op jit(solution)/shard_map/dot_general | solution.py:60
  64.1 56.5 %all-gather.5.cloned.1.call-done = bf16[14336,128]{0,1:T(8,128)(2,1)} async-done(((bf16[3584,128]{0,1:T(8,128)(2,1)}), bf16[14336,128]{0,1:T(8,128)(2,1)}) %all-gather.5.cloned.1.call-update) | async-done | bytes 3670032 | tf_op jit(solution)/shard_map/all_gather | solution.py:40
  120.5 4.9 %fusion.5 = (f32[3584]{0:T(1024)S(1)}, f32[3584]{0:T(1024)S(1)}, f32[3584]{0:T(1024)S(1)}, f32[3584]{0:T(1024)S(1)}, f32[128]{0:T(128)S(1)}, /*index=5*/f32[128]{0:T(128)S(1)}, f32[128]{0:T(128)S(1)}, f32[128]{0:T(128)S(1)}) fusion(f32[3584,512]{0,1:T(8,128)} %convolution_bitcast_fusion, bf16[14336,128]{0,1:T(8,128)(2,1)} %all-gather.5.cloned.1.call-done, ...), kind=kLoop, calls=%fused_computation.16 | loop fusion | flops 9160192 | bytes 11083776 | tf_op jit(solution)/shard_map/reduce_sum | solution.py:70
  125.4 16.7 %all-reduce = (f32[128]{0:T(128)S(1)}, f32[3584]{0:T(1024)S(1)}) all-reduce(f32[128]{0:T(128)S(1)} %multiply_reduce_fusion.4, f32[3584]{0:T(1024)S(1)} %add_add_fusion), channel_id=1, replica_groups=mesh['seq'=8,'tp'=4] {'tp'}, use_global_device_ids=true, to_apply=%region_1.2 | all-reduce | flops 3712 | bytes 29696 | tf_op jit(solution)/shard_map/psum | solution.py:75
  142.1 0.5 broadcast_multiply_fusion.1
  142.7 42.3 %psum.22 = f32[4,128]{1,0:T(4,128)S(1)} all-reduce(f32[4,128]{1,0:T(4,128)S(1)} %pad_maximum_fusion), channel_id=1, replica_groups=mesh['seq'=8,'tp'=4] {'seq','tp'}, use_global_device_ids=true, to_apply=%region_6.7 | all-reduce | flops 512 | bytes 4096 | tf_op jit(solution)/shard_map/psum | solution.py:72
  185.0 0.6 broadcast_multiply_fusion
  185.6 0.5 fusion.16
  (16 shorter events, 0.1 us)
Async XLA Ops:
  7.2 12.7 %copy-start.1 = (bf16[3584,128]{1,0:T(8,128)(2,1)S(1)}, bf16[3584,128]{1,0:T(8,128)(2,1)}, u32[]{:S(2)}) copy-start(bf16[3584,128]{1,0:T(8,128)(2,1)} %param.10) | copy-start | bytes 2752516
  7.2 13.2 %copy-start.2 = (bf16[3584,128]{1,0:T(8,128)(2,1)S(1)}, bf16[3584,128]{1,0:T(8,128)(2,1)}, u32[]{:S(2)}) copy-start(bf16[3584,128]{1,0:T(8,128)(2,1)} %param.9) | copy-start | bytes 2752516
  7.2 42.0 %all-gather.7.cloned.1.call-start = ((), (), s32[]{:S(2)}) async-start(), calls=%async_computation.1 | async-start | bytes 2359296 | tf_op jit(solution)/shard_map/all_gather | solution.py:54
  8.3 8.1 %collective-permute-start.1 = (bf16[64,2048]{1,0:T(8,128)(2,1)S(1)}, bf16[64,2048]{1,0:T(8,128)(2,1)S(1)}, u32[]{:S(2)}, u32[]{:S(2)}) collective-permute-start(bf16[64,2048]{1,0:T(8,128)(2,1)S(1)} %constant_dynamic-slice_fusion.1), channel_id=1, source_target_pairs={{0,16},{4,20},{8,24},{12,28},{16,0},{20,4},{24,8},{28,12},{1,17},{... | collective-permute-start | bytes 786440 | tf_op jit(solution)/shard_map/ppermute | solution.py:11
  18.2 102.3 %all-gather.5.cloned.1.call-start = ((), (), s32[]{:S(2)}) async-start(), calls=%async_computation | async-start | bytes 4587520 | tf_op jit(solution)/shard_map/all_gather | solution.py:40
  18.3 15.9 %collective-permute-start = (bf16[128,2048]{1,0:T(8,128)(2,1)}, bf16[128,2048]{1,0:T(8,128)(2,1)S(1)}, u32[]{:S(2)}, u32[]{:S(2)}) collective-permute-start(bf16[128,2048]{1,0:T(8,128)(2,1)} %param.7), channel_id=1, source_target_pairs={{0,16},{4,20},{8,24},{12,28},{16,0},{20,4},{24,8},{28,12},{1,17},{... | collective-permute-start | bytes 1572872 | tf_op jit(solution)/shard_map/ppermute | solution.py:11
  20.9 1.2 copy-start.4
  22.2 12.0 %copy-start = (bf16[128,2048]{1,0:T(8,128)(2,1)S(1)}, bf16[128,2048]{1,0:T(8,128)(2,1)}, u32[]{:S(2)}) copy-start(bf16[128,2048]{1,0:T(8,128)(2,1)} %param.6) | copy-start | bytes 1572868
  22.2 11.9 %copy-start.3 = (bf16[128,2048]{1,0:T(8,128)(2,1)S(1)}, bf16[128,2048]{1,0:T(8,128)(2,1)}, u32[]{:S(2)}) copy-start(bf16[128,2048]{1,0:T(8,128)(2,1)} %param.7) | copy-start | bytes 1572868
Sparse Core Ops, SparseCore 0:
  18.4 30.8 all-gather.6
  50.8 69.7 all-gather.4
where the time goes:
time: 193 us
  waiting for transfers between devices  87.2 us (45%)
  blocking collectives  59 us (31%)
  matrix products  15.2 us (8%)
  between operations  14.2 us (7%)
  other arithmetic  10.2 us (5%)
  local copies, waits for them, and re-layouts  3.87 us (2%)
  starting transfers between devices  3.25 us (2%)
    all_gather x1, waiting for transfers between devices, shards(): diff_all = lax.all_gather(hidden_diff, 'tp', axis=0)  56.5 us
    psum x1, blocking collectives, shards(): token_total = lax.psum(token_part, ('seq', 'tp'))  42.3 us
    psum x1, blocking collectives, shards(): unit_total, resid_total = lax.psum((unit_part, resid_part), 'tp')  16.7 us
    ppermute x2, waiting for transfers between devices, from_behind(): return lax.ppermute(value, axis, pairs)  16 us
    all_gather x1, waiting for transfers between devices, shards(): grads = lax.all_gather(grad_mean, 'seq', axis=0)  14.7 us
    dot_general x1, matrix products, shards(): lax.dot_general(down_weight, grads, (((1,), (1,)), ((), ())), preferred_e...  13.1 us
    reduce_sum x1, other arithmetic, shards(): unit_part = unit_part + jnp.sum(product, axis=1)  4.87 us
  transfers between devices with their start and end apart: 4, of which 4 were waited for; matrix products, arithmetic and copies ran while one was open for 10% of the time, Pallas kernels for 0%

commit v1 on v0

--- a/solution.py
+++ b/solution.py
@@ -69,7 +69,7 @@
         token_parts.append(jnp.sum(product * in_patch[:, None], axis=0))
         unit_part = unit_part + jnp.sum(product, axis=1)
     token_part = jnp.stack(token_parts)
-    token_total = lax.psum(token_part, ("seq", "tp"))
+    token_total = jnp.sum(lax.all_gather(token_part, ("seq", "tp")), axis=0)
     token_mine = lax.dynamic_index_in_dim(token_total, lax.axis_index("tp"), 0, keepdims=False)
     token_scores = token_mine / math.sqrt(patched.shape[0])
     unit_total, resid_total = lax.psum((unit_part, resid_part), "tp")

time: 193 us -> 218 us (1.13)
  the two profiles are of different devices: /device:TPU:10 before, /device:TPU:0 now
where the time goes in v1:
time: 218 us
  waiting for transfers between devices  89.5 us (41%)
  blocking collectives  80.1 us (37%)
  matrix products  15.2 us (7%)
  between operations  14.2 us (7%)
  other arithmetic  10.2 us (5%)
  starting transfers between devices  4.92 us (2%)
  local copies, waits for them, and re-layouts  3.87 us (2%)
    all_gather x1, blocking collectives, shards(): token_total = jnp.sum(lax.all_gather(token_part, ('seq', 'tp')), axis=0)  63.8 us
    all_gather x1, waiting for transfers between devices, shards(): diff_all = lax.all_gather(hidden_diff, 'tp', axis=0)  58.9 us
    psum x1, blocking collectives, shards(): unit_total, resid_total = lax.psum((unit_part, resid_part), 'tp')  16.2 us
    ppermute x2, waiting for transfers between devices, from_behind(): return lax.ppermute(value, axis, pairs)  15.9 us
    all_gather x1, waiting for transfers between devices, shards(): grads = lax.all_gather(grad_mean, 'seq', axis=0)  14.7 us
    dot_general x1, matrix products, shards(): lax.dot_general(down_weight, grads, (((1,), (1,)), ((), ())), preferred_e...  13.1 us
    reduce_sum x1, other arithmetic, shards(): unit_part = unit_part + jnp.sum(product, axis=1)  4.87 us
    ppermute x2, starting transfers between devices, from_behind(): return lax.ppermute(value, axis, pairs)  4.84 us
  transfers between devices with their start and end apart: 4, of which 4 were waited for; matrix products, arithmetic and copies ran while one was open for 9% of the time, Pallas kernels for 0%

profile of v1, /device:TPU:0, one launch (start us, length us, event | category | flops | bytes accessed | tf_op | source)
XLA Modules:
  0.0 218.0 jit_solution(11252999971586606990)
XLA Ops:
  7.3 1.1 constant_dynamic-slice_fusion.1
  8.3 3.0 %collective-permute-start.1 = (bf16[64,2048]{1,0:T(8,128)(2,1)S(1)}, bf16[64,2048]{1,0:T(8,128)(2,1)S(1)}, u32[]{:S(2)}, u32[]{:S(2)}) collective-permute-start(bf16[64,2048]{1,0:T(8,128)(2,1)S(1)} %constant_dynamic-slice_fusion.1), channel_id=1, source_target_pairs={{0,16},{4,20},{8,24},{12,28},{16,0},{20,4},{24,8},{28,12},{1,17},{... | collective-permute-start | bytes 786440 | tf_op jit(solution)/shard_map/ppermute | solution.py:11
  11.4 6.3 %collective-permute-done.1 = bf16[64,2048]{1,0:T(8,128)(2,1)S(1)} collective-permute-done((bf16[64,2048]{1,0:T(8,128)(2,1)S(1)}, bf16[64,2048]{1,0:T(8,128)(2,1)S(1)}, u32[]{:S(2)}, u32[]{:S(2)}) %collective-permute-start.1) | collective-permute-done | bytes 262176 | tf_op jit(solution)/shard_map/ppermute | solution.py:11
  17.7 1.8 multiply_convert_fusion
  19.5 0.0 all-gather.7.cloned.1.call-start
  19.5 1.8 collective-permute-start
  21.3 0.5 copy.17
  21.9 0.5 copy.16
  22.4 1.1 subtract_convert_fusion
  23.6 0.1 add_select_fusion.1
  23.7 0.3 fusion.22
  24.0 2.1 fusion.8
  26.1 9.6 %collective-permute-done = bf16[128,2048]{1,0:T(8,128)(2,1)S(1)} collective-permute-done((bf16[128,2048]{1,0:T(8,128)(2,1)}, bf16[128,2048]{1,0:T(8,128)(2,1)S(1)}, u32[]{:S(2)}, u32[]{:S(2)}) %collective-permute-start) | collective-permute-done | bytes 524320 | tf_op jit(solution)/shard_map/ppermute | solution.py:11
  35.7 0.4 multiply_reduce_fusion.4
  36.1 14.7 %all-gather.9.cloned.1.call-done = bf16[512,2048]{1,0:T(8,128)(2,1)} async-done(((bf16[64,2048]{1,0:T(8,128)(2,1)}), bf16[512,2048]{1,0:T(8,128)(2,1)}) %all-gather.9.cloned.1.call-update) | async-done | bytes 2097168 | tf_op jit(solution)/shard_map/all_gather | solution.py:54
  50.8 1.7 copy.18
  52.5 13.1 %convolution_bitcast_fusion = f32[3584,512]{0,1:T(8,128)} fusion(bf16[512,2048]{1,0:T(8,128)(2,1)S(1)} %bitcast.22, bf16[3584,2048]{1,0:T(8,128)(2,1)} %param.8), kind=kOutput, calls=%fused_computation.2 | convolution fusion | flops 7516192768 | bytes 24117248 | tf_op jit(solution)/shard_map/dot_general | solution.py:60
  65.6 58.9 %all-gather.7.cloned.1.call-done = bf16[14336,128]{0,1:T(8,128)(2,1)} async-done(((bf16[3584,128]{0,1:T(8,128)(2,1)}), bf16[14336,128]{0,1:T(8,128)(2,1)}) %all-gather.7.cloned.1.call-update) | async-done | bytes 3670032 | tf_op jit(solution)/shard_map/all_gather | solution.py:40
  124.5 4.9 %fusion.5 = (f32[3584]{0:T(1024)S(1)}, f32[3584]{0:T(1024)S(1)}, f32[3584]{0:T(1024)S(1)}, f32[3584]{0:T(1024)S(1)}, f32[128]{0:T(128)S(1)}, /*index=5*/f32[128]{0:T(128)S(1)}, f32[128]{0:T(128)S(1)}, f32[128]{0:T(128)S(1)}) fusion(f32[3584,512]{0,1:T(8,128)} %convolution_bitcast_fusion, bf16[14336,128]{0,1:T(8,128)(2,1)} %all-gather.7.cloned.1.call-done, ...), kind=kLoop, calls=%fused_computation.16 | loop fusion | flops 9160192 | bytes 11083776 | tf_op jit(solution)/shard_map/reduce_sum | solution.py:70
  129.4 16.2 %all-reduce = (f32[128]{0:T(128)S(1)}, f32[3584]{0:T(1024)S(1)}) all-reduce(f32[128]{0:T(128)S(1)} %multiply_reduce_fusion.4, f32[3584]{0:T(1024)S(1)} %add_add_fusion), channel_id=1, replica_groups=mesh['seq'=8,'tp'=4] {'tp'}, use_global_device_ids=true, to_apply=%region_1.2 | all-reduce | flops 3712 | bytes 29696 | tf_op jit(solution)/shard_map/psum | solution.py:75
  145.6 0.5 broadcast_multiply_fusion.1
  146.2 63.8 %all-gather.3 = f32[32,4,128]{2,1,0:T(4,128)S(1)} all-gather(f32[1,4,128]{2,1,0:T(4,128)S(1)} %maximum_bitcast_fusion), channel_id=4, replica_groups=mesh['seq'=8,'tp'=4] {'seq','tp'}, dimensions={0}, use_global_device_ids=true | all-gather | bytes 67584 | tf_op jit(solution)/shard_map/all_gather | solution.py:72
  210.0 0.6 broadcast_multiply_fusion
  210.6 0.5 fusion.16
  (17 shorter events, 0.2 us)
Async XLA Ops:
  7.2 14.2 %copy-start.1 = (bf16[3584,128]{1,0:T(8,128)(2,1)S(1)}, bf16[3584,128]{1,0:T(8,128)(2,1)}, u32[]{:S(2)}) copy-start(bf16[3584,128]{1,0:T(8,128)(2,1)} %param.10) | copy-start | bytes 2752516
  7.2 14.7 %copy-start.2 = (bf16[3584,128]{1,0:T(8,128)(2,1)S(1)}, bf16[3584,128]{1,0:T(8,128)(2,1)}, u32[]{:S(2)}) copy-start(bf16[3584,128]{1,0:T(8,128)(2,1)} %param.9) | copy-start | bytes 2752516
  7.2 43.6 %all-gather.9.cloned.1.call-start = ((), (), s32[]{:S(2)}) async-start(), calls=%async_computation.1 | async-start | bytes 2359296 | tf_op jit(solution)/shard_map/all_gather | solution.py:54
  8.3 9.3 %collective-permute-start.1 = (bf16[64,2048]{1,0:T(8,128)(2,1)S(1)}, bf16[64,2048]{1,0:T(8,128)(2,1)S(1)}, u32[]{:S(2)}, u32[]{:S(2)}) collective-permute-start(bf16[64,2048]{1,0:T(8,128)(2,1)S(1)} %constant_dynamic-slice_fusion.1), channel_id=1, source_target_pairs={{0,16},{4,20},{8,24},{12,28},{16,0},{20,4},{24,8},{28,12},{1,17},{... | collective-permute-start | bytes 786440 | tf_op jit(solution)/shard_map/ppermute | solution.py:11
  19.5 105.0 %all-gather.7.cloned.1.call-start = ((), (), s32[]{:S(2)}) async-start(), calls=%async_computation | async-start | bytes 4587520 | tf_op jit(solution)/shard_map/all_gather | solution.py:40
  19.5 16.2 %collective-permute-start = (bf16[128,2048]{1,0:T(8,128)(2,1)}, bf16[128,2048]{1,0:T(8,128)(2,1)S(1)}, u32[]{:S(2)}, u32[]{:S(2)}) collective-permute-start(bf16[128,2048]{1,0:T(8,128)(2,1)} %param.7), channel_id=1, source_target_pairs={{0,16},{4,20},{8,24},{12,28},{16,0},{20,4},{24,8},{28,12},{1,17},{... | collective-permute-start | bytes 1572872 | tf_op jit(solution)/shard_map/ppermute | solution.py:11
  22.4 1.2 copy-start.4
  23.7 12.1 %copy-start = (bf16[128,2048]{1,0:T(8,128)(2,1)S(1)}, bf16[128,2048]{1,0:T(8,128)(2,1)}, u32[]{:S(2)}) copy-start(bf16[128,2048]{1,0:T(8,128)(2,1)} %param.6) | copy-start | bytes 1572868
  23.7 12.0 %copy-start.3 = (bf16[128,2048]{1,0:T(8,128)(2,1)S(1)}, bf16[128,2048]{1,0:T(8,128)(2,1)}, u32[]{:S(2)}) copy-start(bf16[128,2048]{1,0:T(8,128)(2,1)} %param.7) | copy-start | bytes 1572868
Sparse Core Ops, SparseCore 0:
  19.6 31.1 all-gather.8
  52.4 72.1 all-gather.6
